TPU v7x, 256 devices: a whole 4x4x8 slice. The times are simulated.
256 devices in a mesh: dp: 32 (over z, x), mp: 8 (over y, core).
Axes of the slice: x: 4, y: 4, z: 8, core: 2. Of those that a mesh axis runs over, the one named last changes fastest.
Arguments:
- tokens: bfloat16 [32768, 8192], P('dp', 'mp'), may hold values from -6 to 6
- value_weight: bfloat16 [8192, 1024], P('mp'), may hold values from -0.0625 to 0.0625
- adapter_down_panels: bfloat16 [96, 64, 8192], P('dp', None, 'mp'), may hold values from -0.0625 to 0.0625
- adapter_up_panels: bfloat16 [96, 64, 1024], P('dp', None, 'mp'), may hold values from -0.75 to 0.75
- cotangent: bfloat16 [32768, 1024], P('dp', 'mp'), may hold values from -6 to 6
- block_list_entry: int32 [1024], P('dp'), may hold values from 0 to 31, as said below
- device_tenant_list: int32 [1024], P('dp'), may hold values from 0 to 95, as said below
- tenant_location_map: int32 [96], replicated, may hold values from 0 to 95, as said below
Outputs:
- values: bfloat16 [32768, 1024], P('dp', 'mp')
- token_gradient: bfloat16 [32768, 8192], P('dp', 'mp')
- grad_a: bfloat16 [96, 64, 8192], P('dp', None, 'mp')
- grad_b: bfloat16 [96, 64, 1024], P('dp', None, 'mp')
Inputs may be any that keep to these rules, and one draw needn't show every extreme that they name: `device_tenant_list`: each entry names a tenant; no tenant stands twice in one list. Of one device's 32 entries, at most 2 name tenants whose storage location tenant_location_map[t] lies on one dp index (tenant_location_map[t] // 3), and every device's list has 2 entries on some one dp index. A permutation: tenant t's panels are row tenant_location_map[t] of adapter_down_panels and adapter_up_panels. `block_list_entry`: every entry of a device's tenant list is named by at least one of that device's row blocks.
All inputs are finite; a program needn't handle non-finite values.
Results may differ from a plain program's by a relative error of at most 0.0057.
Values may be sent and summed in bfloat16 or wider, within the bound.
A program may use at most 128 MiB of HBM per device.

v0:
```python
import jax
import jax.numpy as jnp
import numpy as np
from jax import lax
from jax.sharding import Mesh
from jax.sharding import PartitionSpec as P

MOST = 2
DP = ("dz", "dx")


def earlier_same(group):
    count = group.shape[-1]
    ids = jnp.arange(count, dtype=jnp.int32)
    same = (group[..., :, None] == group[..., None, :]) & (ids[:, None] > ids[None, :])
    return jnp.sum(same.astype(jnp.int32), axis=-1)


def shards(
    tokens,
    value_weight,
    adapter_down_panels,
    adapter_up_panels,
    cotangent,
    block_list_entry,
    device_tenant_list,
    tenant_location_map,
):
    rows, width_loc = tokens.shape
    stored, rank, _ = adapter_down_panels.shape
    out_loc = adapter_up_panels.shape[2]
    blocks = block_list_entry.shape[0]
    blk = rows // blocks
    n_z = lax.axis_size("dz")
    n_x = lax.axis_size("dx")
    per_x = min(MOST * n_z, blocks)
    capacity = n_x * per_x
    my_x = lax.axis_index("dx")
    column = n_z * stored
    tenant = jnp.take(device_tenant_list, block_list_entry, mode="clip")
    location = jnp.take(tenant_location_map, tenant, mode="clip")
    owner_x = location // stored % n_x
    position = owner_x * per_x + earlier_same(owner_x)
    slot_ids = jnp.arange(capacity, dtype=jnp.int32)
    block_ids = jnp.arange(blocks, dtype=jnp.int32)
    source = jnp.sum(
        jnp.where(position[None, :] == slot_ids[:, None], block_ids[None, :], 0), axis=1
    )
    x_location = lax.all_gather(location, "dx", axis=0, tiled=False)
    x_owner_x = x_location // stored % n_x
    x_rank = earlier_same(x_owner_x)
    in_column = x_location // stored // n_x * stored + x_location % stored
    mine = x_owner_x == my_x
    slot_panel = (
        jnp.stack(
            [
                jnp.sum(jnp.where(mine & (x_rank == c), in_column + 1, 0), axis=1)
                for c in range(per_x)
            ],
            axis=1,
        ).reshape(capacity)
        - 1
    )
    pick = slot_panel[:, None] == jnp.arange(column, dtype=jnp.int32)[None, :]
    down_col = lax.all_gather(adapter_down_panels, "dz", axis=0, tiled=True)
    up_col = lax.all_gather(adapter_up_panels, "dz", axis=0, tiled=True)
    base_t = lax.psum_scatter(
        lax.dot_general(
            value_weight, tokens, (((0,), (1,)), ((), ())), preferred_element_type=jnp.float32
        ),
        "mp",
        scatter_dimension=0,
        tiled=True,
    )
    cot_full = lax.all_gather(cotangent, "mp", axis=1, tiled=True)
    base_bwd = lax.dot_general(
        cot_full, value_weight, (((1,), (1,)), ((), ())), preferred_element_type=jnp.float32
    )
    token_blocks = tokens.reshape(blocks, blk, width_loc)
    cot_blocks = cotangent.reshape(blocks, blk, out_loc)
    send = jnp.concatenate(
        [jnp.take(token_blocks, source, axis=0), jnp.take(cot_blocks, source, axis=0)], axis=2
    )
    recv = lax.all_to_all(send, "dx", split_axis=0, concat_axis=0, tiled=True)
    tok_recv = recv[:, :, :width_loc]
    cot_recv = recv[:, :, width_loc:]
    panel_at = jnp.clip(slot_panel, 0, column - 1)
    down_sel = jnp.take(down_col, panel_at, axis=0)
    up_sel = jnp.take(up_col, panel_at, axis=0)
    down_part = jnp.einsum("snd,srd->snr", tok_recv, down_sel, preferred_element_type=jnp.float32)
    up_part = jnp.einsum("snc,src->snr", cot_recv, up_sel, preferred_element_type=jnp.float32)
    both = lax.all_gather(
        lax.psum_scatter(
            jnp.stack([down_part, up_part]), "mp", scatter_dimension=1, tiled=True
        ).astype(jnp.bfloat16),
        "mp",
        axis=1,
        tiled=True,
    )
    down_low = both[0]
    up_grad = both[1]
    adapter_out = jnp.einsum("snr,src->snc", down_low, up_sel, preferred_element_type=jnp.float32)
    adapter_bwd = jnp.einsum("snr,srd->snd", up_grad, down_sel, preferred_element_type=jnp.float32)
    back_send = jnp.concatenate(
        [adapter_bwd.astype(jnp.bfloat16), adapter_out.astype(jnp.bfloat16)], axis=2
    )
    back = lax.all_to_all(back_send, "dx", split_axis=0, concat_axis=0, tiled=True)
    pick_rows = jnp.broadcast_to(pick[:, None, :, None], (capacity, blk, column, rank)).reshape(
        capacity * blk, column * rank
    )

    def spread(small):
        wide = jnp.broadcast_to(
            small.reshape(capacity * blk, 1, rank), (capacity * blk, column, rank)
        )
        wide = wide.reshape(capacity * blk, column * rank)
        return jnp.where(pick_rows, wide, jnp.zeros_like(wide))

    grad_a_col = lax.dot_general(
        spread(up_grad),
        tok_recv.reshape(capacity * blk, width_loc),
        (((0,), (0,)), ((), ())),
        preferred_element_type=jnp.float32,
    )
    grad_b_col = lax.dot_general(
        spread(down_low),
        cot_recv.reshape(capacity * blk, out_loc),
        (((0,), (0,)), ((), ())),
        preferred_element_type=jnp.float32,
    )
    grad_a = lax.psum_scatter(grad_a_col, "dz", scatter_dimension=0, tiled=True)
    grad_b = lax.psum_scatter(grad_b_col, "dz", scatter_dimension=0, tiled=True)
    grad_a = grad_a.astype(jnp.bfloat16).reshape(stored, rank, width_loc)
    grad_b = grad_b.astype(jnp.bfloat16).reshape(stored, rank, out_loc)
    mine_back = jnp.take(back, position, axis=0).reshape(rows, width_loc + out_loc)
    values = (base_t.T + mine_back[:, width_loc:].astype(jnp.float32)).astype(jnp.bfloat16)
    token_gradient = (base_bwd + mine_back[:, :width_loc].astype(jnp.float32)).astype(jnp.bfloat16)
    return (values, token_gradient, grad_a, grad_b)


def split_dp(mesh):
    devices = np.asarray(mesh.devices)
    n_dp, n_mp = devices.shape
    try:
        n_x = len({tuple(d.coords)[0] for d in devices[:, 0]})
    except (AttributeError, TypeError):
        n_x = 1
    if n_x < 1 or n_dp % n_x:
        n_x = 1
    return Mesh(devices.reshape(n_dp // n_x, n_x, n_mp), ("dz", "dx", "mp"))


def solution(mesh):
    in_specs = (
        P(DP, "mp"),
        P("mp", None),
        P(DP, None, "mp"),
        P(DP, None, "mp"),
        P(DP, "mp"),
        P(DP),
        P(DP),
        P(),
    )
    out_specs = (P(DP, "mp"), P(DP, "mp"), P(DP, None, "mp"), P(DP, None, "mp"))
    return jax.shard_map(
        shards, mesh=split_dp(mesh), in_specs=in_specs, out_specs=out_specs, check_vma=False
    )
```

profile of v0, /device:TPU:1, one launch (start us, length us, event | category | flops | bytes accessed | tf_op | source)
XLA Modules:
  0.0 417.1 jit_solution(15197474575198803912)
XLA Ops:
  22.0 5.1 %all-to-all-start = ((bf16[64,32,1152]{2,1,0:T(8,128)(2,1)}), bf16[64,32,1152]{2,1,0:T(8,128)(2,1)}, u32[]{:S(2)}, u32[]{:S(2)}) async-start(bf16[64,32,1152]{2,1,0:T(8,128)(2,1)} %pad_maximum_fusion), calls=%async_computation.1 | async-start | bytes 9437184 | tf_op jit(solution)/shard_map/all_to_all | solution.py:84
  28.8 53.5 %all-reduce = s32[128]{0:T(128)S(1)} all-reduce(s32[128]{0:T(128)S(1)} %dynamic-update-slice), channel_id=2, replica_groups=mesh['dz'=8,'dx'=4,'mp'=8] {'dx'}, use_global_device_ids=true, to_apply=%add | all-reduce | flops 128 | bytes 1024
  85.0 24.2 %all_gather.18 = bf16[24,64,128]{2,1,0:T(8,128)(2,1)S(1)} all-gather(bf16[3,64,128]{2,1,0:T(8,128)(2,1)S(1)} %copy-done.5), channel_id=1, replica_groups=mesh['dz'=8,'dx'=4,'mp'=8] {'dz'}, dimensions={0}, use_global_device_ids=true | all-gather | bytes 442368 | tf_op jit(solution)/shard_map/all_gather | solution.py:66
  112.7 7.3 %gather_fusion.4 = bf16[64,64,1024]{2,1,0:T(8,128)(2,1)} fusion(bf16[24,64,1024]{2,1,0:T(8,128)(2,1)} %all-gather.4.cloned.1.call-done, s32[1024]{0:T(1024)S(1)} %pad_clamp_fusion.1), kind=kCustom, calls=%fused_computation.4 | custom fusion | bytes 16777472 | tf_op jit(solution)/shard_map/jit(_take)/gather | solution.py:88
  120.0 7.1 %fusion.3 = f32[1,64,32,64]{3,2,1,0:T(8,128)S(1)} fusion(bf16[64,64,1024]{2,1,0:T(8,128)(2,1)} %gather_fusion.4, pred[64]{0:T(512)(128)(4,1)S(1)} %compare_and_fusion, bf16[64,32,1152]{2,1,0:T(8,128)(2,1)} %all-to-all-done), kind=kOutput, calls=%fused_computation.20 | convolution fusion | flops 272629760 | bytes 13107264 | tf_op jit(solution)/shard_map/snd,srd->snr/dot_general | solution.py:90
  128.7 2.9 reshape.353
  133.6 34.9 %reduce-scatter.13.cloned.1.call-done = f32[8,4096]{1,0:T(8,128)} async-done(((f32[64,4096]{1,0:T(8,128)}), f32[8,4096]{1,0:T(8,128)}) %reduce-scatter.13.cloned.1.call-update) | async-done | bytes 131088
  169.7 17.0 %all_gather.19 = bf16[2,64,32,64]{3,2,1,0:T(8,128)(2,1)S(1)} all-gather(bf16[2,8,32,64]{3,2,1,0:T(8,128)(2,1)S(1)} %copy.69), channel_id=1, replica_groups=mesh['dz'=8,'dx'=4,'mp'=8] {'mp'}, dimensions={1}, use_global_device_ids=true | all-gather | bytes 589824 | tf_op jit(solution)/shard_map/all_gather | solution.py:92
  187.7 9.4 %broadcast_select_fusion = (bf16[64,32,24,64]{3,2,1,0:T(8,128)(2,1)}, bf16[64,32,24,64]{3,2,1,0:T(8,128)(2,1)}) fusion(pred[64,24]{1,0:T(8,128)(4,1)S(1)} %iota_compare_fusion, bf16[64,32,64]{2,1,0:T(8,128)(2,1)S(1)} %get-tuple-element.42, bf16[64,32,64]{2,1,0:T(8,128)(2,1)S(1)} %get-tuple-element.43), kind=kLoop, calls=%fused_computation.7 | loop fusion | flops 6291456 | bytes 13108736 | tf_op jit(solution)/shard_map/jit(_where)/select_n | solution.py:117
  197.1 16.8 %select_n.261 = bf16[2048,1536]{1,0:T(8,128)(2,1)} reshape(bf16[64,32,24,64]{3,2,1,0:T(8,128)(2,1)} %get-tuple-element.44) | data formatting | bytes 12582912 | tf_op jit(solution)/shard_map/jit(_where)/select_n | solution.py:117
  213.9 5.6 %fusion.24 = f32[1536,128]{1,0:T(8,128)} fusion(bf16[2048,1536]{1,0:T(8,128)(2,1)} %select_n.261, bf16[2048,128]{1,0:T(8,128)(2,1)} %bitcast.82), kind=kOutput, calls=%fused_computation.112 | convolution fusion | flops 805306368 | bytes 7602176 | tf_op jit(solution)/shard_map/dot_general | solution.py:125
  220.1 6.0 %fusion.22 = f32[1024,1024]{1,0:T(8,128)} fusion(bf16[1024,1024]{1,0:T(8,128)(2,1)} %param.9, bf16[1024,1024]{1,0:T(8,128)(2,1)S(1)} %copy-done), kind=kOutput, calls=%fused_computation.110 | convolution fusion | flops 2147483648 | bytes 8388608 | tf_op jit(solution)/shard_map/dot_general | solution.py:68
  226.4 5.0 %slice.38 = bf16[64,32,1024]{2,1,0:T(8,128)(2,1)} slice(bf16[64,32,1152]{2,1,0:T(8,128)(2,1)} %all-to-all-done), slice={[0:64], [0:32], [0:1024]} | slice | bytes 8388608 | tf_op jit(solution)/shard_map/slice | solution.py:85
  231.5 16.9 %select_n.259 = bf16[2048,1536]{1,0:T(8,128)(2,1)} reshape(bf16[64,32,24,64]{3,2,1,0:T(8,128)(2,1)} %get-tuple-element.45) | data formatting | bytes 12582912 | tf_op jit(solution)/shard_map/jit(_where)/select_n | solution.py:117
  248.4 11.8 %fusion.23 = f32[1536,1024]{1,0:T(8,128)} fusion(bf16[2048,1536]{1,0:T(8,128)(2,1)} %select_n.259, bf16[2048,1024]{1,0:T(8,128)(2,1)} %bitcast.80), kind=kOutput, calls=%fused_computation.111 | convolution fusion | flops 6442450944 | bytes 16777216 | tf_op jit(solution)/shard_map/dot_general | solution.py:119
  261.9 4.7 %fusion.2 = bf16[64,32,1024]{2,1,0:T(8,128)(2,1)S(1)} fusion(bf16[64,64,1024]{2,1,0:T(8,128)(2,1)} %gather_fusion.4, pred[64]{0:T(512)(128)(4,1)S(1)} %compare_and_fusion, bf16[2,64,32,64]{3,2,1,0:T(8,128)(2,1)S(1)} %copy-done.3), kind=kOutput, calls=%fused_computation.16 | convolution fusion | flops 274726912 | bytes 13107712 | tf_op jit(solution)/shard_map/snr,srd->snd/dot_general | solution.py:103
  269.5 5.1 %all-to-all-start.1 = ((bf16[64,32,1152]{2,1,0:T(8,128)(2,1)}), bf16[64,32,1152]{2,1,0:T(8,128)(2,1)}, u32[]{:S(2)}, u32[]{:S(2)}) async-start(bf16[64,32,1152]{2,1,0:T(8,128)(2,1)} %pad_maximum_fusion.1), calls=%async_computation.2 | async-start | bytes 9437184 | tf_op jit(solution)/shard_map/all_to_all | solution.py:107
  276.3 52.7 %all-to-all-done.1 = bf16[64,32,1152]{2,1,0:T(8,128)(2,1)} async-done(((bf16[64,32,1152]{2,1,0:T(8,128)(2,1)}), bf16[64,32,1152]{2,1,0:T(8,128)(2,1)}, u32[]{:S(2)}, u32[]{:S(2)}) %all-to-all-start.1) | async-done | bytes 4718624 | tf_op jit(solution)/shard_map/all_to_all | solution.py:107
  329.0 4.6 %gather_fusion.6 = bf16[32,32,1152]{2,1,0:T(8,128)(2,1)} fusion(bf16[64,32,1152]{2,1,0:T(8,128)(2,1)} %all-to-all-done.1, s32[1024]{0:T(1024)S(1)} %pad_clamp_fusion), kind=kCustom, calls=%fused_computation.6 | custom fusion | bytes 4718720 | tf_op jit(solution)/shard_map/jit(_take)/gather | solution.py:135
  333.6 4.3 %copy.60 = bf16[1024,1152]{0,1:T(8,128)(2,1)} copy(bf16[1024,1152]{1,0:T(8,128)(2,1)} %bitcast.79) | data formatting | bytes 4718592 | tf_op jit(solution)/shard_map/jit(_take)/gather | solution.py:135
  337.9 3.3 broadcast_select_fusion.8
  341.2 6.7 %add_convert_fusion = bf16[1024,1024]{0,1:T(8,128)(2,1)} fusion(bf16[1024,1152]{0,1:T(8,128)(2,1)} %broadcast_select_fusion.8, bf16[1024,1024]{1,0:T(8,128)(2,1)} %all-gather.6.cloned.1.call-done, bf16[1024,1024]{1,0:T(8,128)(2,1)} %param.9), kind=kOutput, calls=%fused_computation.12 | convolution fusion | flops 2150629376 | bytes 8388608 | tf_op jit(solution)/shard_map/dot_general | solution.py:76
  348.0 3.9 copy.63
  353.9 54.4 %reduce-scatter.9.cloned.1.call-done = f32[192,1024]{1,0:T(8,128)} async-done(((f32[1536,1024]{1,0:T(8,128)}), f32[192,1024]{1,0:T(8,128)}) %reduce-scatter.9.cloned.1.call-update) | async-done | bytes 786448 | tf_op jit(solution)/shard_map/reduce_scatter | solution.py:131
  (106 shorter events, 38.7 us)
Async XLA Ops:
  7.2 6.6 %copy-start = (bf16[1024,1024]{1,0:T(8,128)(2,1)S(1)}, bf16[1024,1024]{1,0:T(8,128)(2,1)}, u32[]{:S(2)}) copy-start(bf16[1024,1024]{1,0:T(8,128)(2,1)} %param.8) | copy-start | bytes 6291460
  7.2 105.5 %all-gather.4.cloned.1.call-start = ((), (), s32[]{:S(2)}) async-start(), calls=%async_computation.7 | async-start | bytes 3538944 | tf_op jit(solution)/shard_map/all_gather | solution.py:65
  11.3 17.2 %copy-start.6 = (s32[32]{0:T(128)}, s32[32]{0:T(128)S(1)}, u32[]{:S(2)}) copy-start(s32[32]{0:T(128)S(1)} %gather_fusion.1) | copy-start | bytes 388
  22.0 5.2 %copy-start.9 = (u32[256]{0:T(256)S(1)}, u32[256]{0:T(256)}, u32[]{:S(2)}) copy-start(u32[256]{0:T(256)} %constant.169) | copy-start | bytes 3076
  22.0 62.9 %copy-start.5 = (bf16[3,64,128]{2,1,0:T(8,128)(2,1)S(1)}, bf16[3,64,128]{2,1,0:T(8,128)(2,1)}, u32[]{:S(2)}) copy-start(bf16[3,64,128]{2,1,0:T(8,128)(2,1)} %param.11) | copy-start | bytes 147460
  22.0 87.9 %all-to-all-start = ((bf16[64,32,1152]{2,1,0:T(8,128)(2,1)}), bf16[64,32,1152]{2,1,0:T(8,128)(2,1)}, u32[]{:S(2)}, u32[]{:S(2)}) async-start(bf16[64,32,1152]{2,1,0:T(8,128)(2,1)} %pad_maximum_fusion), calls=%async_computation.1 | async-start | bytes 9437184 | tf_op jit(solution)/shard_map/all_to_all | solution.py:84
  27.2 141.4 %reduce-scatter.13.cloned.1.call-start = ((), (), s32[]{:S(2)}) async-start(), calls=%async_computation.11 | async-start | bytes 1179648
  120.0 7.1 %copy-start.4 = (f32[1,64,32,64]{3,2,1,0:T(8,128)S(1)}, f32[1,64,32,64]{3,2,1,0:T(8,128)}, u32[]{:S(2)}) copy-start(f32[1,64,32,64]{3,2,1,0:T(8,128)} %convolution_bitcast_fusion) | copy-start | bytes 1572868
  131.6 143.2 %reduce-scatter.11.cloned.1.call-start = ((), (), s32[]{:S(2)}) async-start(), calls=%async_computation.10 | async-start | bytes 884736 | tf_op jit(solution)/shard_map/reduce_scatter | solution.py:132
  186.6 1.0 copy-start.2
  219.5 121.7 %all-gather.6.cloned.1.call-start = ((), (), s32[]{:S(2)}) async-start(), calls=%async_computation.8 | async-start | bytes 2359296 | tf_op jit(solution)/shard_map/all_gather | solution.py:75
  220.1 131.8 %reduce-scatter.7.cloned.1.call-start = ((), (), s32[]{:S(2)}) async-start(), calls=%async_computation.6 | async-start | bytes 4718592 | tf_op jit(solution)/shard_map/reduce_scatter | solution.py:67
  226.2 182.2 %reduce-scatter.9.cloned.1.call-start = ((), (), s32[]{:S(2)}) async-start(), calls=%async_computation.9 | async-start | bytes 7077888 | tf_op jit(solution)/shard_map/reduce_scatter | solution.py:131
  260.2 1.2 copy-start.3
  269.5 5.3 %copy-start.7 = (s32[32]{0:T(128)S(1)}, s32[32]{0:T(128)}, u32[]{:S(2)}) copy-start(s32[32]{0:T(128)} %copy-done.6) | copy-start | bytes 388
  269.5 5.3 %copy-start.8 = (s32[32]{0:T(128)S(1)}, s32[32]{0:T(128)}, u32[]{:S(2)}) copy-start(s32[32]{0:T(128)} %get-tuple-element.39) | copy-start | bytes 388
  269.5 59.5 %all-to-all-start.1 = ((bf16[64,32,1152]{2,1,0:T(8,128)(2,1)}), bf16[64,32,1152]{2,1,0:T(8,128)(2,1)}, u32[]{:S(2)}, u32[]{:S(2)}) async-start(bf16[64,32,1152]{2,1,0:T(8,128)(2,1)} %pad_maximum_fusion.1), calls=%async_computation.2 | async-start | bytes 9437184 | tf_op jit(solution)/shard_map/all_to_all | solution.py:107
  341.2 69.0 %copy-start.1 = (bf16[1024,1024]{1,0:T(8,128)(2,1)S(1)}, bf16[1024,1024]{1,0:T(8,128)(2,1)}, u32[]{:S(2)}) copy-start(bf16[1024,1024]{1,0:T(8,128)(2,1)} %param.8) | copy-start | bytes 6291460
Sparse Core Ops, SparseCore 0:
  9.8 48.5 all-gather.3
  131.7 36.7 reduce-scatter.12
  219.6 32.7 reduce-scatter.10
  254.3 33.2 all-gather.5
  290.1 39.1 reduce-scatter.6
  331.9 76.4 reduce-scatter.8
where the time goes:
time: 419 us; the launch traced here: 417 us
  waiting for transfers between devices  143 us (34%)
  blocking collectives  94.7 us (23%)
  local copies, waits for them, and re-layouts  78.8 us (19%)
  matrix products  45.2 us (11%)
  other arithmetic  29.5 us (7%)
  between operations  15 us (4%)
  starting transfers between devices  10.7 us (3%)
    reduce_scatter x1, waiting for transfers between devices, shards(): grad_a = lax.psum_scatter(grad_a_col, 'dz', scatter_dimension=0, tiled=True)  54.4 us
    unnamed x1, blocking collectives  53.5 us
    all_to_all x1, waiting for transfers between devices, shards(): lax.all_to_all(back_send, 'dx', split_axis=0, concat_axis=0, tiled=True)  52.7 us
    unnamed x7, waiting for transfers between devices  36.2 us
    select_n x2, local copies, waits for them, and re-layouts, spread(): return jnp.where(pick_rows, wide, jnp.zeros_like(wide))  33.8 us
    all_gather x1, blocking collectives, shards(): up_col = lax.all_gather(adapter_up_panels, 'dz', axis=0, tiled=True)  24.2 us
    all_gather x1, blocking collectives, shards(): lax.all_gather(lax.psum_scatter(jnp.stack([down_part, up_part]), 'mp', sc...  17 us
    dot_general x1, matrix products, shards(): lax.dot_general(spread(up_grad), tok_recv.reshape(capacity * blk, width_l...  11.8 us
  transfers between devices with their start and end apart: 8, of which 3 were waited for; matrix products, arithmetic and copies ran while one was open for 23% of the time, Pallas kernels for 0%

commit v1 on v0

--- a/solution.py
+++ b/solution.py
@@ -63,7 +63,9 @@
     )
     pick = slot_panel[:, None] == jnp.arange(column, dtype=jnp.int32)[None, :]
     down_col = lax.all_gather(adapter_down_panels, "dz", axis=0, tiled=True)
-    up_col = lax.all_gather(adapter_up_panels, "dz", axis=0, tiled=True)
+    up_col = jnp.concatenate(
+        lax.all_to_all(jnp.stack([adapter_up_panels] * lax.axis_size("dz")), "dz", 0, 0), axis=0
+    )
     base_t = lax.psum_scatter(
         lax.dot_general(
             value_weight, tokens, (((0,), (1,)), ((), ())), preferred_element_type=jnp.float32

time: 419 us -> 406 us (0.969)
  blocking collectives: 94.7 us -> 71 us
  starting transfers between devices: 10.7 us -> 19.7 us
  other arithmetic: 29.5 us -> 34.2 us
    all_gather x1 -> x0, blocking collectives: 24.2 us -> none  [shards(): up_col = lax.all_gather(adapter_up_panels, 'dz', axis=0, tiled=True)]
    all_to_all x0 -> x1, starting transfers between devices: none -> 9.01 us  [shards(): lax.all_to_all(jnp.stack([adapter_up_panels] * lax.axis_size('dz')), 'dz'...]
    unnamed x28 -> x30, local copies, waits for them, and re-layouts: 11.8 us -> 11.8 us
  transfers between devices with their start and end apart: 8 -> 9, of which waited for: 3 -> 3; matrix products, arithmetic and copies ran while one was open for 23% -> 25% of each run, Pallas kernels for 0% -> 0%
where the time goes in v1:
time: 406 us; the launch traced here: 404 us
  waiting for transfers between devices  140 us (34%)
  local copies, waits for them, and re-layouts  79.6 us (20%)
  blocking collectives  71 us (17%)
  matrix products  45.1 us (11%)
  other arithmetic  34.2 us (8%)
  starting transfers between devices  19.7 us (5%)
  between operations  15 us (4%)
    reduce_scatter x1, waiting for transfers between devices, shards(): grad_a = lax.psum_scatter(grad_a_col, 'dz', scatter_dimension=0, tiled=True)  54.5 us
    unnamed x1, blocking collectives  54 us
    all_to_all x1, waiting for transfers between devices, shards(): lax.all_to_all(back_send, 'dx', split_axis=0, concat_axis=0, tiled=True)  52.7 us
    select_n x2, local copies, waits for them, and re-layouts, spread(): return jnp.where(pick_rows, wide, jnp.zeros_like(wide))  33.8 us
    unnamed x7, waiting for transfers between devices  32.6 us
    all_gather x1, blocking collectives, shards(): lax.all_gather(lax.psum_scatter(jnp.stack([down_part, up_part]), 'mp', sc...  17 us
    dot_general x1, matrix products, shards(): lax.dot_general(spread(up_grad), tok_recv.reshape(capacity * blk, width_l...  11.8 us
    unnamed x30, local copies, waits for them, and re-layouts  11.8 us
  transfers between devices with their start and end apart: 9, of which 3 were waited for; matrix products, arithmetic and copies ran while one was open for 25% of the time, Pallas kernels for 0%

profile of v1, /device:TPU:1, one launch (start us, length us, event | category | flops | bytes accessed | tf_op | source)
XLA Modules:
  0.0 404.3 jit_solution(11780823363085790427)
XLA Ops:
  9.6 9.0 %all-to-all-start.1 = ((bf16[8,3,64,128]{3,2,1,0:T(8,128)(2,1)}), bf16[8,3,64,128]{3,2,1,0:T(8,128)(2,1)S(1)}, u32[]{:S(2)}, u32[]{:S(2)}) async-start(bf16[8,3,64,128]{3,2,1,0:T(8,128)(2,1)} %stack.89), calls=%async_computation.2 | async-start | bytes 786432 | tf_op jit(solution)/shard_map/all_to_all | solution.py:67
  25.6 4.7 %broadcast_select_fusion.3 = bf16[64,32,1024]{2,1,0:T(8,128)(2,1)} fusion(bf16[64,32,1024]{2,1,0:T(8,128)(2,1)} %gather_fusion.2, pred[64]{0:T(512)(128)(4,1)S(1)} %compare_and_fusion.1), kind=kLoop, calls=%fused_computation.13 | loop fusion | flops 2097152 | bytes 8388672 | tf_op jit(solution)/shard_map/jit(_take)/select_n | solution.py:84
  31.1 5.0 %pad_maximum_fusion = bf16[64,32,1152]{2,1,0:T(8,128)(2,1)} fusion(bf16[64,32,128]{2,1,0:T(8,128)(2,1)S(1)} %broadcast_select_fusion.12, bf16[64,32,1024]{2,1,0:T(8,128)(2,1)} %broadcast_select_fusion.3), kind=kLoop, calls=%fused_computation.10 | loop fusion | flops 9437184 | bytes 9437184 | tf_op jit(solution)/shard_map/concatenate | solution.py:83
  36.1 5.1 %all-to-all-start = ((bf16[64,32,1152]{2,1,0:T(8,128)(2,1)}), bf16[64,32,1152]{2,1,0:T(8,128)(2,1)}, u32[]{:S(2)}, u32[]{:S(2)}) async-start(bf16[64,32,1152]{2,1,0:T(8,128)(2,1)} %pad_maximum_fusion), calls=%async_computation.1 | async-start | bytes 9437184 | tf_op jit(solution)/shard_map/all_to_all | solution.py:86
  42.8 54.0 %all-reduce = s32[128]{0:T(128)S(1)} all-reduce(s32[128]{0:T(128)S(1)} %dynamic-update-slice), channel_id=2, replica_groups=mesh['dz'=8,'dx'=4,'mp'=8] {'dx'}, use_global_device_ids=true, to_apply=%add | all-reduce | flops 128 | bytes 1024
  103.5 7.3 %gather_fusion.4 = bf16[64,64,1024]{2,1,0:T(8,128)(2,1)} fusion(bf16[24,64,1024]{2,1,0:T(8,128)(2,1)} %all-gather.4.cloned.1.call-done, s32[1024]{0:T(1024)S(1)} %pad_clamp_fusion.1), kind=kCustom, calls=%fused_computation.4 | custom fusion | bytes 16777472 | tf_op jit(solution)/shard_map/jit(_take)/gather | solution.py:90
  110.8 7.1 %fusion.3 = f32[1,64,32,64]{3,2,1,0:T(8,128)S(1)} fusion(bf16[64,64,1024]{2,1,0:T(8,128)(2,1)} %gather_fusion.4, pred[64]{0:T(512)(128)(4,1)S(1)} %copy-done.9, bf16[64,32,1152]{2,1,0:T(8,128)(2,1)} %all-to-all-done), kind=kOutput, calls=%fused_computation.20 | convolution fusion | flops 272629760 | bytes 13107264 | tf_op jit(solution)/shard_map/snd,srd->snr/dot_general | solution.py:92
  124.4 31.3 %reduce-scatter.13.cloned.1.call-done = f32[8,4096]{1,0:T(8,128)} async-done(((f32[64,4096]{1,0:T(8,128)}), f32[8,4096]{1,0:T(8,128)}) %reduce-scatter.13.cloned.1.call-update) | async-done | bytes 131088
  156.9 17.0 %all_gather.15 = bf16[2,64,32,64]{3,2,1,0:T(8,128)(2,1)S(1)} all-gather(bf16[2,8,32,64]{3,2,1,0:T(8,128)(2,1)S(1)} %copy.69), channel_id=1, replica_groups=mesh['dz'=8,'dx'=4,'mp'=8] {'mp'}, dimensions={1}, use_global_device_ids=true | all-gather | bytes 589824 | tf_op jit(solution)/shard_map/all_gather | solution.py:94
  174.9 9.4 %broadcast_select_fusion = (bf16[64,32,24,64]{3,2,1,0:T(8,128)(2,1)}, bf16[64,32,24,64]{3,2,1,0:T(8,128)(2,1)}) fusion(pred[64,24]{1,0:T(8,128)(4,1)S(1)} %iota_compare_fusion, bf16[64,32,64]{2,1,0:T(8,128)(2,1)S(1)} %get-tuple-element.42, bf16[64,32,64]{2,1,0:T(8,128)(2,1)S(1)} %get-tuple-element.43), kind=kLoop, calls=%fused_computation.7 | loop fusion | flops 6291456 | bytes 13108736 | tf_op jit(solution)/shard_map/jit(_where)/select_n | solution.py:119
  184.3 16.8 %select_n.261 = bf16[2048,1536]{1,0:T(8,128)(2,1)} reshape(bf16[64,32,24,64]{3,2,1,0:T(8,128)(2,1)} %get-tuple-element.44) | data formatting | bytes 12582912 | tf_op jit(solution)/shard_map/jit(_where)/select_n | solution.py:119
  201.1 5.6 %fusion.24 = f32[1536,128]{1,0:T(8,128)} fusion(bf16[2048,1536]{1,0:T(8,128)(2,1)} %select_n.261, bf16[2048,128]{1,0:T(8,128)(2,1)} %bitcast.84), kind=kOutput, calls=%fused_computation.112 | convolution fusion | flops 805306368 | bytes 7602176 | tf_op jit(solution)/shard_map/dot_general | solution.py:127
  207.3 6.0 %fusion.22 = f32[1024,1024]{1,0:T(8,128)} fusion(bf16[1024,1024]{1,0:T(8,128)(2,1)} %param.9, bf16[1024,1024]{1,0:T(8,128)(2,1)S(1)} %copy-done), kind=kOutput, calls=%fused_computation.110 | convolution fusion | flops 2147483648 | bytes 8388608 | tf_op jit(solution)/shard_map/dot_general | solution.py:70
  213.6 5.0 %slice.38 = bf16[64,32,1024]{2,1,0:T(8,128)(2,1)} slice(bf16[64,32,1152]{2,1,0:T(8,128)(2,1)} %all-to-all-done), slice={[0:64], [0:32], [0:1024]} | slice | bytes 8388608 | tf_op jit(solution)/shard_map/slice | solution.py:87
  218.7 16.9 %select_n.259 = bf16[2048,1536]{1,0:T(8,128)(2,1)} reshape(bf16[64,32,24,64]{3,2,1,0:T(8,128)(2,1)} %get-tuple-element.45) | data formatting | bytes 12582912 | tf_op jit(solution)/shard_map/jit(_where)/select_n | solution.py:119
  235.6 11.8 %fusion.23 = f32[1536,1024]{1,0:T(8,128)} fusion(bf16[2048,1536]{1,0:T(8,128)(2,1)} %select_n.259, bf16[2048,1024]{1,0:T(8,128)(2,1)} %bitcast.82), kind=kOutput, calls=%fused_computation.111 | convolution fusion | flops 6442450944 | bytes 16777216 | tf_op jit(solution)/shard_map/dot_general | solution.py:121
  249.1 4.7 %fusion.2 = bf16[64,32,1024]{2,1,0:T(8,128)(2,1)S(1)} fusion(bf16[64,64,1024]{2,1,0:T(8,128)(2,1)} %gather_fusion.4, pred[64]{0:T(512)(128)(4,1)S(1)} %copy-done.9, bf16[2,64,32,64]{3,2,1,0:T(8,128)(2,1)S(1)} %copy-done.3), kind=kOutput, calls=%fused_computation.16 | convolution fusion | flops 274726912 | bytes 13107712 | tf_op jit(solution)/shard_map/snr,srd->snd/dot_general | solution.py:105
  256.6 5.1 %all-to-all-start.2 = ((bf16[64,32,1152]{2,1,0:T(8,128)(2,1)}), bf16[64,32,1152]{2,1,0:T(8,128)(2,1)}, u32[]{:S(2)}, u32[]{:S(2)}) async-start(bf16[64,32,1152]{2,1,0:T(8,128)(2,1)} %pad_maximum_fusion.1), calls=%async_computation.3 | async-start | bytes 9437184 | tf_op jit(solution)/shard_map/all_to_all | solution.py:109
  263.5 52.7 %all-to-all-done.2 = bf16[64,32,1152]{2,1,0:T(8,128)(2,1)} async-done(((bf16[64,32,1152]{2,1,0:T(8,128)(2,1)}), bf16[64,32,1152]{2,1,0:T(8,128)(2,1)}, u32[]{:S(2)}, u32[]{:S(2)}) %all-to-all-start.2) | async-done | bytes 4718624 | tf_op jit(solution)/shard_map/all_to_all | solution.py:109
  316.2 4.6 %gather_fusion.6 = bf16[32,32,1152]{2,1,0:T(8,128)(2,1)} fusion(bf16[64,32,1152]{2,1,0:T(8,128)(2,1)} %all-to-all-done.2, s32[1024]{0:T(1024)S(1)} %pad_clamp_fusion), kind=kCustom, calls=%fused_computation.6 | custom fusion | bytes 4718720 | tf_op jit(solution)/shard_map/jit(_take)/gather | solution.py:137
  320.8 4.3 %copy.60 = bf16[1024,1152]{0,1:T(8,128)(2,1)} copy(bf16[1024,1152]{1,0:T(8,128)(2,1)} %bitcast.80) | data formatting | bytes 4718592 | tf_op jit(solution)/shard_map/jit(_take)/gather | solution.py:137
  328.4 6.7 %add_convert_fusion = bf16[1024,1024]{0,1:T(8,128)(2,1)} fusion(bf16[1024,1152]{0,1:T(8,128)(2,1)} %broadcast_select_fusion.8, bf16[1024,1024]{1,0:T(8,128)(2,1)} %all-gather.6.cloned.1.call-done, bf16[1024,1024]{1,0:T(8,128)(2,1)} %param.9), kind=kOutput, calls=%fused_computation.12 | convolution fusion | flops 2150629376 | bytes 8388608 | tf_op jit(solution)/shard_map/dot_general | solution.py:78
  335.1 3.9 copy.63
  341.1 54.5 %reduce-scatter.9.cloned.1.call-done = f32[192,1024]{1,0:T(8,128)} async-done(((f32[1536,1024]{1,0:T(8,128)}), f32[192,1024]{1,0:T(8,128)}) %reduce-scatter.9.cloned.1.call-update) | async-done | bytes 786448 | tf_op jit(solution)/shard_map/reduce_scatter | solution.py:133
  (110 shorter events, 40.8 us)
Async XLA Ops:
  7.2 15.6 %copy-start = (bf16[1024,1024]{1,0:T(8,128)(2,1)S(1)}, bf16[1024,1024]{1,0:T(8,128)(2,1)}, u32[]{:S(2)}) copy-start(bf16[1024,1024]{1,0:T(8,128)(2,1)} %param.8) | copy-start | bytes 6291460
  7.2 96.3 %all-gather.4.cloned.1.call-start = ((), (), s32[]{:S(2)}) async-start(), calls=%async_computation.8 | async-start | bytes 3538944 | tf_op jit(solution)/shard_map/all_gather | solution.py:65
  9.6 26.5 %all-to-all-start.1 = ((bf16[8,3,64,128]{3,2,1,0:T(8,128)(2,1)}), bf16[8,3,64,128]{3,2,1,0:T(8,128)(2,1)S(1)}, u32[]{:S(2)}, u32[]{:S(2)}) async-start(bf16[8,3,64,128]{3,2,1,0:T(8,128)(2,1)} %stack.89), calls=%async_computation.2 | async-start | bytes 786432 | tf_op jit(solution)/shard_map/all_to_all | solution.py:67
  21.9 20.6 %copy-start.6 = (s32[32]{0:T(128)}, s32[32]{0:T(128)S(1)}, u32[]{:S(2)}) copy-start(s32[32]{0:T(128)S(1)} %gather_fusion.1) | copy-start | bytes 388
  25.6 4.7 %copy-start.5 = (bf16[1024,128]{1,0:T(8,128)(2,1)S(1)}, bf16[1024,128]{1,0:T(8,128)(2,1)}, u32[]{:S(2)}) copy-start(bf16[1024,128]{1,0:T(8,128)(2,1)} %param.12) | copy-start | bytes 786436
  36.1 5.2 %copy-start.10 = (u32[256]{0:T(256)S(1)}, u32[256]{0:T(256)}, u32[]{:S(2)}) copy-start(u32[256]{0:T(256)} %constant.169) | copy-start | bytes 3076
  36.1 64.7 %all-to-all-start = ((bf16[64,32,1152]{2,1,0:T(8,128)(2,1)}), bf16[64,32,1152]{2,1,0:T(8,128)(2,1)}, u32[]{:S(2)}, u32[]{:S(2)}) async-start(bf16[64,32,1152]{2,1,0:T(8,128)(2,1)} %pad_maximum_fusion), calls=%async_computation.1 | async-start | bytes 9437184 | tf_op jit(solution)/shard_map/all_to_all | solution.py:86
  41.2 114.6 %reduce-scatter.13.cloned.1.call-start = ((), (), s32[]{:S(2)}) async-start(), calls=%async_computation.12 | async-start | bytes 1179648
  103.5 7.3 %copy-start.9 = (pred[64]{0:T(512)(128)(4,1)S(1)}, pred[64]{0:T(512)(128)(4,1)}, u32[]{:S(2)}) copy-start(pred[64]{0:T(512)(128)(4,1)} %compare_and_fusion) | copy-start | bytes 196
  110.8 7.1 %copy-start.4 = (f32[1,64,32,64]{3,2,1,0:T(8,128)S(1)}, f32[1,64,32,64]{3,2,1,0:T(8,128)}, u32[]{:S(2)}) copy-start(f32[1,64,32,64]{3,2,1,0:T(8,128)} %convolution_bitcast_fusion) | copy-start | bytes 1572868
  122.4 139.5 %reduce-scatter.11.cloned.1.call-start = ((), (), s32[]{:S(2)}) async-start(), calls=%async_computation.11 | async-start | bytes 884736 | tf_op jit(solution)/shard_map/reduce_scatter | solution.py:134
  173.8 1.0 copy-start.2
  206.7 121.7 %all-gather.6.cloned.1.call-start = ((), (), s32[]{:S(2)}) async-start(), calls=%async_computation.9 | async-start | bytes 2359296 | tf_op jit(solution)/shard_map/all_gather | solution.py:77
  207.3 131.8 %reduce-scatter.7.cloned.1.call-start = ((), (), s32[]{:S(2)}) async-start(), calls=%async_computation.7 | async-start | bytes 4718592 | tf_op jit(solution)/shard_map/reduce_scatter | solution.py:69
  213.3 182.2 %reduce-scatter.9.cloned.1.call-start = ((), (), s32[]{:S(2)}) async-start(), calls=%async_computation.10 | async-start | bytes 7077888 | tf_op jit(solution)/shard_map/reduce_scatter | solution.py:133
  247.4 1.2 copy-start.3
  256.6 5.3 %copy-start.7 = (s32[32]{0:T(128)S(1)}, s32[32]{0:T(128)}, u32[]{:S(2)}) copy-start(s32[32]{0:T(128)} %copy-done.6) | copy-start | bytes 388
  256.6 5.3 %copy-start.8 = (s32[32]{0:T(128)S(1)}, s32[32]{0:T(128)}, u32[]{:S(2)}) copy-start(s32[32]{0:T(128)} %get-tuple-element.39) | copy-start | bytes 388
  256.6 59.5 %all-to-all-start.2 = ((bf16[64,32,1152]{2,1,0:T(8,128)(2,1)}), bf16[64,32,1152]{2,1,0:T(8,128)(2,1)}, u32[]{:S(2)}, u32[]{:S(2)}) async-start(bf16[64,32,1152]{2,1,0:T(8,128)(2,1)} %pad_maximum_fusion.1), calls=%async_computation.3 | async-start | bytes 9437184 | tf_op jit(solution)/shard_map/all_to_all | solution.py:109
  328.4 69.1 %copy-start.1 = (bf16[1024,1024]{1,0:T(8,128)(2,1)S(1)}, bf16[1024,1024]{1,0:T(8,128)(2,1)}, u32[]{:S(2)}) copy-start(bf16[1024,1024]{1,0:T(8,128)(2,1)} %param.8) | copy-start | bytes 6291460
Sparse Core Ops, SparseCore 0:
  9.8 50.7 all-gather.3
  122.5 33.1 reduce-scatter.12
  206.8 32.8 reduce-scatter.10
  241.5 33.2 all-gather.5
  277.3 39.1 reduce-scatter.6
  319.1 76.4 reduce-scatter.8
